TPU v7x, 128 devices: a whole 4x4x4 slice. The times are simulated.
128 devices in a mesh: rows: 64 (over x, y_hi, z, core), grp: 2 (over y_lo).
Axes of the slice: x: 4, y: 4 (y_hi: 2, y_lo: 2; y = y_hi * 2 + y_lo), z: 4, core: 2. Of those that a mesh axis runs over, the one named last changes fastest.
Arguments:
- snapshots: float32 [524288, 256], P(('rows', 'grp'))
- blocks: bfloat16 [4096, 16, 128, 128], P(('rows', 'grp')), may hold values from -96 to 96
- columns: int32 [4096, 16], P(('rows', 'grp')), may hold values from 0 to 63
Outputs:
- projected: float32 [256, 256], replicated
- scaled_factor: float32 [256, 256], replicated
Inputs may be any that keep to these rules, and one draw needn't show every extreme that they name: `columns`: each stored block couples its block row to a block row of the same group of 2 * 32 consecutive block rows.
All inputs are finite; a program needn't handle non-finite values.
Results may differ from a plain program's by a relative error of at most 0.003.
Values may be sent and summed in bfloat16 or wider, within the bound.
No kernel may reach another device: no remote copies, remote signals or barrier semaphores. Data moves between devices by JAX's collectives and lax.ppermute only.
A program may use at most 192 MiB of HBM per device.

v0:
```python
import math
import jax
import jax.numpy as jnp
from jax import lax
from jax.sharding import PartitionSpec as P


def from_partner(value, axis, stride):
    mask = 2**stride
    pairs = [(source, source ^ mask) for source in range(lax.axis_size(axis))]
    return lax.ppermute(value, axis, pairs)


def inner_gram(left, right):
    return lax.dot_general(
        left,
        right,
        (((0,), (0,)), ((), ())),
        precision=lax.Precision.HIGHEST,
        preferred_element_type=jnp.float32,
    )


def upper_inverse(factor):
    size = factor.shape[0]
    unit_rows = jnp.eye(size, dtype=factor.dtype)

    def substitute(count, inverse):
        index = (size - 1 - count).astype(jnp.int32)
        frow = lax.dynamic_slice_in_dim(factor, index, 1, 0)
        unit = lax.dynamic_slice_in_dim(unit_rows, index, 1, 0)
        pivot = lax.dynamic_slice(factor, (index, index), (1, 1))
        fresh = (unit - jnp.dot(frow, inverse, precision=lax.Precision.HIGHEST)) / pivot
        return lax.dynamic_update_slice_in_dim(inverse, fresh, index, 0)

    return lax.fori_loop(jnp.int32(0), jnp.int32(size), substitute, jnp.zeros_like(factor))


def local(snapshots, blocks, columns):
    local_gram = inner_gram(snapshots, snapshots)
    factor = jnp.linalg.cholesky(local_gram).T
    levels = lax.axis_size(("rows", "grp")).bit_length() - 1
    for bit in range(levels):
        partner = from_partner(factor, ("rows", "grp"), bit)
        combined = inner_gram(factor, factor) + inner_gram(partner, partner)
        factor = jnp.linalg.cholesky(combined).T
    inverse = upper_inverse(factor)
    basis = jnp.dot(snapshots, inverse, precision=lax.Precision.HIGHEST)
    basis_half = basis.astype(jnp.bfloat16)
    block_len = blocks.shape[2]
    width = snapshots.shape[1]
    gathered = lax.all_gather(basis_half, "grp", axis=0, tiled=True)
    window = gathered.reshape(gathered.shape[0] // block_len, block_len, width)
    picked = jnp.take(window, columns, axis=0)
    image = jnp.einsum("bjrc,bjck->brk", blocks, picked, preferred_element_type=jnp.float32)
    image = image.reshape(snapshots.shape[0], width)
    partial_terms = inner_gram(basis, image)
    projected = lax.psum(partial_terms, ("rows", "grp"))
    total_rows = snapshots.shape[0] * lax.axis_size(("rows", "grp"))
    scaled_factor = factor / math.sqrt(total_rows)
    return (projected, scaled_factor)


def solution(mesh):
    return jax.shard_map(
        local,
        mesh=mesh,
        in_specs=(
            P(("rows", "grp"), None),
            P(("rows", "grp"), None, None, None),
            P(("rows", "grp"), None),
        ),
        out_specs=(P(), P()),
        check_vma=False,
    )
```

profile of v0, /device:TPU:1, one launch (start us, length us, event | category | flops | bytes accessed | tf_op | source)
XLA Modules:
  0.0 1051.1 jit_solution(15019776480115702252)
XLA Ops:
  7.2 10.4 fusion.133
  17.8 11.7 %cholesky.382 = f32[128,128]{1,0:T(8,128)S(1)} custom-call(f32[128,128]{1,0:T(8,128)S(1)} %cholesky.650), custom_call_target="Cholesky" | custom-call | tf_op jit(solution)/shard_map/jit(cholesky)/cholesky | solution.py:41
  29.5 9.8 custom-call.15
  39.8 11.7 %cholesky.399 = f32[128,128]{1,0:T(8,128)S(1)} custom-call(f32[128,128]{1,0:T(8,128)S(1)} %convolution_subtract_fusion.1), custom_call_target="Cholesky" | custom-call | tf_op jit(solution)/shard_map/jit(cholesky)/cholesky | solution.py:41
  63.3 11.7 %cholesky.416 = f32[128,128]{1,0:T(8,128)S(1)} custom-call(f32[128,128]{1,0:T(8,128)S(1)} %cholesky.653), custom_call_target="Cholesky" | custom-call | tf_op jit(solution)/shard_map/jit(cholesky)/cholesky | solution.py:46
  75.7 9.8 custom-call.16
  86.7 11.7 %cholesky.433 = f32[128,128]{1,0:T(8,128)S(1)} custom-call(f32[128,128]{1,0:T(8,128)S(1)} %slice_subtract_fusion.6), custom_call_target="Cholesky" | custom-call | tf_op jit(solution)/shard_map/jit(cholesky)/cholesky | solution.py:46
  106.7 11.7 %cholesky.450 = f32[128,128]{1,0:T(8,128)S(1)} custom-call(f32[128,128]{1,0:T(8,128)S(1)} %cholesky.656), custom_call_target="Cholesky" | custom-call | tf_op jit(solution)/shard_map/jit(cholesky)/cholesky | solution.py:46
  119.2 9.8 custom-call.17
  130.1 11.7 %cholesky.467 = f32[128,128]{1,0:T(8,128)S(1)} custom-call(f32[128,128]{1,0:T(8,128)S(1)} %slice_subtract_fusion.5), custom_call_target="Cholesky" | custom-call | tf_op jit(solution)/shard_map/jit(cholesky)/cholesky | solution.py:46
  155.6 11.7 %cholesky.484 = f32[128,128]{1,0:T(8,128)S(1)} custom-call(f32[128,128]{1,0:T(8,128)S(1)} %cholesky.659), custom_call_target="Cholesky" | custom-call | tf_op jit(solution)/shard_map/jit(cholesky)/cholesky | solution.py:46
  168.1 9.8 custom-call.18
  179.0 11.7 %cholesky.501 = f32[128,128]{1,0:T(8,128)S(1)} custom-call(f32[128,128]{1,0:T(8,128)S(1)} %slice_subtract_fusion.4), custom_call_target="Cholesky" | custom-call | tf_op jit(solution)/shard_map/jit(cholesky)/cholesky | solution.py:46
  205.0 11.7 %cholesky.518 = f32[128,128]{1,0:T(8,128)S(1)} custom-call(f32[128,128]{1,0:T(8,128)S(1)} %cholesky.662), custom_call_target="Cholesky" | custom-call | tf_op jit(solution)/shard_map/jit(cholesky)/cholesky | solution.py:46
  217.5 9.8 custom-call.19
  228.4 11.7 %cholesky.535 = f32[128,128]{1,0:T(8,128)S(1)} custom-call(f32[128,128]{1,0:T(8,128)S(1)} %slice_subtract_fusion.3), custom_call_target="Cholesky" | custom-call | tf_op jit(solution)/shard_map/jit(cholesky)/cholesky | solution.py:46
  253.2 11.7 %cholesky.552 = f32[128,128]{1,0:T(8,128)S(1)} custom-call(f32[128,128]{1,0:T(8,128)S(1)} %cholesky.665), custom_call_target="Cholesky" | custom-call | tf_op jit(solution)/shard_map/jit(cholesky)/cholesky | solution.py:46
  265.7 9.8 custom-call.20
  276.6 11.7 %cholesky.569 = f32[128,128]{1,0:T(8,128)S(1)} custom-call(f32[128,128]{1,0:T(8,128)S(1)} %slice_subtract_fusion.2), custom_call_target="Cholesky" | custom-call | tf_op jit(solution)/shard_map/jit(cholesky)/cholesky | solution.py:46
  299.0 11.7 %cholesky.586 = f32[128,128]{1,0:T(8,128)S(1)} custom-call(f32[128,128]{1,0:T(8,128)S(1)} %cholesky.668), custom_call_target="Cholesky" | custom-call | tf_op jit(solution)/shard_map/jit(cholesky)/cholesky | solution.py:46
  311.4 9.8 custom-call.21
  322.4 11.7 %cholesky.603 = f32[128,128]{1,0:T(8,128)S(1)} custom-call(f32[128,128]{1,0:T(8,128)S(1)} %slice_subtract_fusion.1), custom_call_target="Cholesky" | custom-call | tf_op jit(solution)/shard_map/jit(cholesky)/cholesky | solution.py:46
  346.0 11.7 %cholesky.620 = f32[128,128]{1,0:T(8,128)S(1)} custom-call(f32[128,128]{1,0:T(8,128)S(1)} %cholesky.671), custom_call_target="Cholesky" | custom-call | tf_op jit(solution)/shard_map/jit(cholesky)/cholesky | solution.py:46
  357.8 9.8 custom-call.22
  368.0 11.7 %cholesky.637 = f32[128,128]{1,0:T(8,128)S(1)} custom-call(f32[128,128]{1,0:T(8,128)S(1)} %slice_subtract_fusion), custom_call_target="Cholesky" | custom-call | tf_op jit(solution)/shard_map/jit(cholesky)/cholesky | solution.py:46
  382.7 388.4 %while.12 = (s32[]{:T(128)}, f32[256,256]{1,0:T(8,128)S(1)}, f32[256,256]{1,0:T(8,128)S(1)}, f32[256,256]{1,0:T(8,128)S(1)}, s32[]{:T(128)}, /*index=5*/s32[]{:T(128)}, s32[]{:T(128)}, s32[]{:T(128)}) while((s32[]{:T(128)}, f32[256,256]{1,0:T(8,128)S(1)}, f32[256,256]{1,0:T(8,128)S(1)}, f32[256,256]{1,0:T(8,128)S(1)}, s32[]{:T(128)}, ...), condition=%wide.region_5.7_spmd, body=%wide.region_4.6_spmd.sunk | while | flops 786950 | bytes 268439 | solution.py:36
  771.1 8.6 fusion.134
  783.7 64.5 %all-gather.2.cloned.1.call-done = bf16[8192,256]{0,1:T(8,128)(2,1)} async-done(((bf16[4096,256]{0,1:T(8,128)(2,1)}), bf16[8192,256]{0,1:T(8,128)(2,1)}) %all-gather.2.cloned.1.call-update) | async-done | bytes 4194320 | tf_op jit(solution)/shard_map/all_gather | solution.py:52
  854.5 18.3 %gather_fusion = bf16[512,128,256]{2,1,0:T(8,128)(2,1)} fusion(bf16[64,128,256]{2,1,0:T(8,128)(2,1)} %bitcast.165, s32[1024]{0:T(1024)S(1)} %pad_clamp_fusion), kind=kCustom, calls=%fused_computation | custom fusion | bytes 67110912 | tf_op jit(solution)/shard_map/jit(_take)/gather | solution.py:54
  872.8 20.2 %fusion.4 = f32[32,256,128,1]{1,2,3,0:T(8,128)} fusion(bf16[32,16,128,128]{3,2,1,0:T(8,128)(2,1)} %param.7, bf16[32,16,128,256]{3,2,1,0:T(8,128)(2,1)} %bitcast.166, pred[32,16]{1,0:T(8,128)(4,1)S(1)} %copy.54), kind=kOutput, calls=%fused_computation.6 | convolution fusion | flops 4311744512 | bytes 54526464 | tf_op jit(solution)/shard_map/bjrc,bjck->brk/dot_general | solution.py:55
  893.1 6.6 fusion.135
  900.5 141.9 %all-reduce.3.cloned.1.call-done = f32[256,256]{1,0:T(8,128)} async-done(((f32[256,256]{1,0:T(8,128)}), f32[256,256]{1,0:T(8,128)}) %all-reduce.3.cloned.1.call-update) | async-done | bytes 262160 | tf_op jit(solution)/shard_map/psum | solution.py:58
  (908 shorter events, 482.0 us)
Async XLA Ops:
  7.2 841.0 %all-gather.2.cloned.1.call-start = ((), (), s32[]{:S(2)}) async-start(), calls=%async_computation | async-start | bytes 6291456 | tf_op jit(solution)/shard_map/all_gather | solution.py:52
  51.6 2.1 copy-start.2
  54.7 8.0 collective-permute-start
  102.7 3.4 collective-permute-start.1
  146.1 8.9 collective-permute-start.2
  195.1 9.3 collective-permute-start.3
  244.4 8.2 collective-permute-start.4
  292.6 5.7 collective-permute-start.5
  338.4 7.0 collective-permute-start.6
  779.7 2.0 copy-start
  781.7 1.7 copy-start.3
  783.4 259.0 %all-reduce.3.cloned.1.call-start = ((), (), s32[]{:S(2)}) async-start(), calls=%async_computation.1 | async-start | bytes 524288 | tf_op jit(solution)/shard_map/psum | solution.py:58
  872.8 20.2 %copy-start.1 = (f32[256,4096]{1,0:T(8,128)S(1)}, f32[256,4096]{1,0:T(8,128)}, u32[]{:S(2)}) copy-start(f32[256,4096]{1,0:T(8,128)} %copy-done) | copy-start | bytes 12582916
Sparse Core Ops, SparseCore 0:
  783.5 64.6 all-gather.1
  899.8 142.5 all-reduce.2
where the time goes:
time: 1070 us; the launch traced here: 1050 us
  other arithmetic  289 us (27%)
  matrix products  279 us (26%)
  waiting for transfers between devices  229 us (21%)
  local copies, waits for them, and re-layouts  203 us (19%)
  between operations  25.5 us (2%)
  starting transfers between devices  17.9 us (2%)
    another operation x49, other arithmetic, local(): factor = jnp.linalg.cholesky(combined).T  246 us
    dot_general x256, matrix products, substitute(): jnp.dot(frow, inverse, precision=lax.Precision.HIGHEST)  213 us
    dynamic_slice x256, local copies, waits for them, and re-layouts, substitute(): pivot = lax.dynamic_slice(factor, (index, index), (1, 1))  152 us
    psum x1, waiting for transfers between devices, local(): projected = lax.psum(partial_terms, ('rows', 'grp'))  142 us
    all_gather x1, waiting for transfers between devices, local(): gathered = lax.all_gather(basis_half, 'grp', axis=0, tiled=True)  64.5 us
    another operation x6, other arithmetic, local(): factor = jnp.linalg.cholesky(local_gram).T  34 us
    dot_general x16, matrix products, inner_gram(): lax.dot_general(left, right, (((0,), (0,)), ((), ())), precision=lax.Prec...  29.9 us
    ppermute x7, waiting for transfers between devices, from_partner(): return lax.ppermute(value, axis, pairs)  22.4 us
  transfers between devices with their start and end apart: 9, of which 8 were waited for; matrix products, arithmetic and copies ran while one was open for 1% of the time, Pallas kernels for 0%

commit v1 on v0

--- a/solution.py
+++ b/solution.py
@@ -55,7 +55,7 @@
     image = jnp.einsum("bjrc,bjck->brk", blocks, picked, preferred_element_type=jnp.float32)
     image = image.reshape(snapshots.shape[0], width)
     partial_terms = inner_gram(basis, image)
-    projected = lax.psum(partial_terms, ("rows", "grp"))
+    projected = lax.psum(lax.psum(partial_terms, "rows"), "grp")
     total_rows = snapshots.shape[0] * lax.axis_size(("rows", "grp"))
     scaled_factor = factor / math.sqrt(total_rows)
     return (projected, scaled_factor)

time: 1070 us -> 1540 us (1.44)
  waiting for transfers between devices: 229 us -> 707 us
    psum x1 -> x2, waiting for transfers between devices: 142 us -> 620 us  [local(): projected = lax.psum(lax.psum(partial_terms, 'rows'), 'grp')]
  transfers between devices with their start and end apart: 9 -> 10, of which waited for: 8 -> 9; matrix products, arithmetic and copies ran while one was open for 1% -> 1% of each run, Pallas kernels for 0% -> 0%
where the time goes in v1:
time: 1540 us; the launch traced here: 1530 us
  waiting for transfers between devices  707 us (46%)
  other arithmetic  289 us (19%)
  matrix products  279 us (18%)
  local copies, waits for them, and re-layouts  203 us (13%)
  between operations  25.3 us (2%)
  starting transfers between devices  18 us (1%)
    psum x2, waiting for transfers between devices, local(): projected = lax.psum(lax.psum(partial_terms, 'rows'), 'grp')  620 us
    another operation x49, other arithmetic, local(): factor = jnp.linalg.cholesky(combined).T  246 us
    dot_general x256, matrix products, substitute(): jnp.dot(frow, inverse, precision=lax.Precision.HIGHEST)  213 us
    dynamic_slice x256, local copies, waits for them, and re-layouts, substitute(): pivot = lax.dynamic_slice(factor, (index, index), (1, 1))  152 us
    all_gather x1, waiting for transfers between devices, local(): gathered = lax.all_gather(basis_half, 'grp', axis=0, tiled=True)  64.5 us
    another operation x6, other arithmetic, local(): factor = jnp.linalg.cholesky(local_gram).T  34 us
  transfers between devices with their start and end apart: 10, of which 9 were waited for; matrix products, arithmetic and copies ran while one was open for 1% of the time, Pallas kernels for 0%

profile of v1, /device:TPU:1, one launch (start us, length us, event | category | flops | bytes accessed | tf_op | source)
XLA Modules:
  0.0 1529.3 jit_solution(8149049296241948254)
XLA Ops:
  7.2 10.4 fusion.133
  17.8 11.7 cholesky.382
  29.5 9.8 custom-call.15
  39.8 11.7 cholesky.399
  63.3 11.7 cholesky.416
  75.7 9.8 custom-call.16
  86.7 11.7 cholesky.433
  106.7 11.7 cholesky.450
  119.2 9.8 custom-call.17
  130.1 11.7 cholesky.467
  155.6 11.7 cholesky.484
  168.1 9.8 custom-call.18
  179.0 11.7 cholesky.501
  205.0 11.7 cholesky.518
  217.5 9.8 custom-call.19
  228.4 11.7 cholesky.535
  253.2 11.7 cholesky.552
  265.7 9.8 custom-call.20
  276.6 11.7 cholesky.569
  299.0 11.7 cholesky.586
  311.4 9.8 custom-call.21
  322.4 11.7 cholesky.603
  346.0 11.7 cholesky.620
  357.8 9.8 custom-call.22
  368.0 11.7 cholesky.637
  382.7 388.4 %while.12 = (s32[]{:T(128)}, f32[256,256]{1,0:T(8,128)S(1)}, f32[256,256]{1,0:T(8,128)S(1)}, f32[256,256]{1,0:T(8,128)S(1)}, s32[]{:T(128)}, /*index=5*/s32[]{:T(128)}, s32[]{:T(128)}, s32[]{:T(128)}) while((s32[]{:T(128)}, f32[256,256]{1,0:T(8,128)S(1)}, f32[256,256]{1,0:T(8,128)S(1)}, f32[256,256]{1,0:T(8,128)S(1)}, s32[]{:T(128)}, ...), condition=%wide.region_5.7_spmd, body=%wide.region_4.6_spmd.sunk | while | flops 786950 | bytes 268439 | solution.py:36
  771.1 8.6 fusion.134
  783.7 64.5 %all-gather.2.cloned.1.call-done = bf16[8192,256]{0,1:T(8,128)(2,1)} async-done(((bf16[4096,256]{0,1:T(8,128)(2,1)}), bf16[8192,256]{0,1:T(8,128)(2,1)}) %all-gather.2.cloned.1.call-update) | async-done | bytes 4194320 | tf_op jit(solution)/shard_map/all_gather | solution.py:52
  854.5 18.3 %gather_fusion = bf16[512,128,256]{2,1,0:T(8,128)(2,1)} fusion(bf16[64,128,256]{2,1,0:T(8,128)(2,1)} %bitcast.165, s32[1024]{0:T(1024)S(1)} %pad_clamp_fusion), kind=kCustom, calls=%fused_computation | custom fusion | bytes 67110912 | tf_op jit(solution)/shard_map/jit(_take)/gather | solution.py:54
  872.8 20.2 %fusion.4 = f32[32,256,128,1]{1,2,3,0:T(8,128)} fusion(bf16[32,16,128,128]{3,2,1,0:T(8,128)(2,1)} %param.7, bf16[32,16,128,256]{3,2,1,0:T(8,128)(2,1)} %bitcast.166, pred[32,16]{1,0:T(8,128)(4,1)S(1)} %copy.54), kind=kOutput, calls=%fused_computation.6 | convolution fusion | flops 4311744512 | bytes 54526464 | tf_op jit(solution)/shard_map/bjrc,bjck->brk/dot_general | solution.py:55
  899.7 590.1 %all-reduce.4.cloned.1.call-done = f32[256,256]{1,0:T(8,128)} async-done(((f32[256,256]{1,0:T(8,128)}), f32[256,256]{1,0:T(8,128)}) %all-reduce.4.cloned.1.call-update) | async-done | bytes 262160 | tf_op jit(solution)/shard_map/psum | solution.py:58
  1490.7 30.2 %all-reduce.6.cloned.1.call-done = f32[256,256]{1,0:T(8,128)} async-done(((f32[256,256]{1,0:T(8,128)}), f32[256,256]{1,0:T(8,128)}) %all-reduce.6.cloned.1.call-update) | async-done | bytes 262160 | tf_op jit(solution)/shard_map/psum | solution.py:58
  (911 shorter events, 488.6 us)
Async XLA Ops:
  7.2 841.0 %all-gather.2.cloned.1.call-start = ((), (), s32[]{:S(2)}) async-start(), calls=%async_computation | async-start | bytes 6291456 | tf_op jit(solution)/shard_map/all_gather | solution.py:52
  51.6 2.1 copy-start.2
  54.7 8.0 collective-permute-start
  102.7 3.4 collective-permute-start.1
  146.1 8.9 collective-permute-start.2
  195.1 9.3 collective-permute-start.3
  244.4 8.2 collective-permute-start.4
  292.6 5.7 collective-permute-start.5
  338.4 7.0 collective-permute-start.6
  779.7 2.0 copy-start
  781.7 1.7 copy-start.3
  783.4 706.4 %all-reduce.4.cloned.1.call-start = ((), (), s32[]{:S(2)}) async-start(), calls=%async_computation.1 | async-start | bytes 524288 | tf_op jit(solution)/shard_map/psum | solution.py:58
  872.8 20.2 %copy-start.1 = (f32[256,4096]{1,0:T(8,128)S(1)}, f32[256,4096]{1,0:T(8,128)}, u32[]{:S(2)}) copy-start(f32[256,4096]{1,0:T(8,128)} %copy-done) | copy-start | bytes 12582916
  899.7 621.3 %all-reduce.6.cloned.1.call-start = ((), (), s32[]{:S(2)}) async-start(), calls=%async_computation.2 | async-start | bytes 524288 | tf_op jit(solution)/shard_map/psum | solution.py:58
Sparse Core Ops, SparseCore 0:
  783.5 64.6 all-gather.1
  899.8 589.9 all-reduce.3
  1492.4 28.4 all-reduce.5

commit v2 on v0

--- a/solution.py
+++ b/solution.py
@@ -55,7 +55,7 @@
     image = jnp.einsum("bjrc,bjck->brk", blocks, picked, preferred_element_type=jnp.float32)
     image = image.reshape(snapshots.shape[0], width)
     partial_terms = inner_gram(basis, image)
-    projected = lax.psum(partial_terms, ("rows", "grp"))
+    projected = jnp.sum(lax.all_gather(partial_terms, ("rows", "grp")), axis=0)
     total_rows = snapshots.shape[0] * lax.axis_size(("rows", "grp"))
     scaled_factor = factor / math.sqrt(total_rows)
     return (projected, scaled_factor)

time: 1070 us -> 1280 us (1.20)
  waiting for transfers between devices: 229 us -> 436 us
  other arithmetic: 289 us -> 302 us
    all_gather x0 -> x1, waiting for transfers between devices: none -> 349 us  [local(): projected = jnp.sum(lax.all_gather(partial_terms, ('rows', 'grp')), axis=0)]
    psum x1 -> x0, waiting for transfers between devices: 142 us -> none  [local(): projected = lax.psum(partial_terms, ('rows', 'grp'))]
where the time goes in v2:
time: 1280 us; the launch traced here: 1270 us
  waiting for transfers between devices  436 us (34%)
  other arithmetic  302 us (24%)
  matrix products  279 us (22%)
  local copies, waits for them, and re-layouts  202 us (16%)
  between operations  25.5 us (2%)
  starting transfers between devices  17.9 us (1%)
    all_gather x1, waiting for transfers between devices, local(): projected = jnp.sum(lax.all_gather(partial_terms, ('rows', 'grp')), axis=0)  349 us
    another operation x49, other arithmetic, local(): factor = jnp.linalg.cholesky(combined).T  246 us
    dot_general x256, matrix products, substitute(): jnp.dot(frow, inverse, precision=lax.Precision.HIGHEST)  213 us
    dynamic_slice x256, local copies, waits for them, and re-layouts, substitute(): pivot = lax.dynamic_slice(factor, (index, index), (1, 1))  152 us
    all_gather x1, waiting for transfers between devices, local(): gathered = lax.all_gather(basis_half, 'grp', axis=0, tiled=True)  64.5 us
    another operation x6, other arithmetic, local(): factor = jnp.linalg.cholesky(local_gram).T  34 us
    dot_general x16, matrix products, inner_gram(): lax.dot_general(left, right, (((0,), (0,)), ((), ())), precision=lax.Prec...  29.9 us
  transfers between devices with their start and end apart: 9, of which 8 were waited for; matrix products, arithmetic and copies ran while one was open for 1% of the time, Pallas kernels for 0%

profile of v2, /device:TPU:1, one launch (start us, length us, event | category | flops | bytes accessed | tf_op | source)
XLA Modules:
  0.0 1269.4 jit_solution(11715629049904712082)
XLA Ops:
  7.2 10.4 fusion.133
  17.8 11.7 cholesky.382
  29.5 9.8 custom-call.15
  39.8 11.7 cholesky.399
  63.3 11.7 cholesky.416
  75.7 9.8 custom-call.16
  86.7 11.7 cholesky.433
  106.7 11.7 cholesky.450
  119.2 9.8 custom-call.17
  130.1 11.7 cholesky.467
  155.6 11.7 cholesky.484
  168.1 9.8 custom-call.18
  179.0 11.7 cholesky.501
  205.0 11.7 cholesky.518
  217.5 9.8 custom-call.19
  228.4 11.7 cholesky.535
  253.2 11.7 cholesky.552
  265.7 9.8 custom-call.20
  276.6 11.7 cholesky.569
  299.0 11.7 cholesky.586
  311.4 9.8 custom-call.21
  322.4 11.7 cholesky.603
  346.0 11.7 cholesky.620
  357.8 9.8 custom-call.22
  368.0 11.7 cholesky.637
  382.7 388.4 %while.12 = (s32[]{:T(128)}, f32[256,256]{1,0:T(8,128)S(1)}, f32[256,256]{1,0:T(8,128)S(1)}, f32[256,256]{1,0:T(8,128)S(1)}, s32[]{:T(128)}, /*index=5*/s32[]{:T(128)}, s32[]{:T(128)}, s32[]{:T(128)}) while((s32[]{:T(128)}, f32[256,256]{1,0:T(8,128)S(1)}, f32[256,256]{1,0:T(8,128)S(1)}, f32[256,256]{1,0:T(8,128)S(1)}, s32[]{:T(128)}, ...), condition=%wide.region_5.7_spmd, body=%wide.region_4.6_spmd.sunk | while | flops 786950 | bytes 268439 | solution.py:36
  771.1 8.6 fusion.134
  783.7 64.5 %all-gather.4.cloned.1.call-done = bf16[8192,256]{0,1:T(8,128)(2,1)} async-done(((bf16[4096,256]{0,1:T(8,128)(2,1)}), bf16[8192,256]{0,1:T(8,128)(2,1)}) %all-gather.4.cloned.1.call-update) | async-done | bytes 4194320 | tf_op jit(solution)/shard_map/all_gather | solution.py:52
  854.5 18.3 %gather_fusion = bf16[512,128,256]{2,1,0:T(8,128)(2,1)} fusion(bf16[64,128,256]{2,1,0:T(8,128)(2,1)} %bitcast.166, s32[1024]{0:T(1024)S(1)} %pad_clamp_fusion), kind=kCustom, calls=%fused_computation | custom fusion | bytes 67110912 | tf_op jit(solution)/shard_map/jit(_take)/gather | solution.py:54
  872.8 20.2 %fusion.4 = f32[32,256,128,1]{1,2,3,0:T(8,128)} fusion(bf16[32,16,128,128]{3,2,1,0:T(8,128)(2,1)} %param.7, bf16[32,16,128,256]{3,2,1,0:T(8,128)(2,1)} %bitcast.167, pred[32,16]{1,0:T(8,128)(4,1)S(1)} %copy.54), kind=kOutput, calls=%fused_computation.6 | convolution fusion | flops 4311744512 | bytes 54526464 | tf_op jit(solution)/shard_map/bjrc,bjck->brk/dot_general | solution.py:55
  900.5 349.2 %all-gather.6.cloned.1.call-done = f32[32768,256]{1,0:T(8,128)} async-done(((f32[256,256]{1,0:T(8,128)}), f32[32768,256]{1,0:T(8,128)}) %all-gather.6.cloned.1.call-update) | async-done | bytes 33554448 | tf_op jit(solution)/shard_map/all_gather | solution.py:58
  1249.7 12.7 reduce_sum.9
  (908 shorter events, 486.9 us)
Async XLA Ops:
  7.2 841.0 %all-gather.4.cloned.1.call-start = ((), (), s32[]{:S(2)}) async-start(), calls=%async_computation | async-start | bytes 6291456 | tf_op jit(solution)/shard_map/all_gather | solution.py:52
  51.6 2.1 copy-start.2
  54.7 8.0 collective-permute-start
  102.7 3.4 collective-permute-start.1
  146.1 8.9 collective-permute-start.2
  195.1 9.3 collective-permute-start.3
  244.4 8.2 collective-permute-start.4
  292.6 5.7 collective-permute-start.5
  338.4 7.0 collective-permute-start.6
  779.7 2.0 copy-start
  781.7 1.7 copy-start.3
  783.4 466.3 %all-gather.6.cloned.1.call-start = ((), (), s32[]{:S(2)}) async-start(), calls=%async_computation.1 | async-start | bytes 33816576 | tf_op jit(solution)/shard_map/all_gather | solution.py:58
  872.8 20.2 %copy-start.1 = (f32[256,4096]{1,0:T(8,128)S(1)}, f32[256,4096]{1,0:T(8,128)}, u32[]{:S(2)}) copy-start(f32[256,4096]{1,0:T(8,128)} %copy-done) | copy-start | bytes 12582916
Sparse Core Ops, SparseCore 0:
  783.5 64.6 all-gather.3
  899.8 349.8 all-gather.5
